TPU v7x, 256 devices: a whole 4x4x8 slice. The times are simulated.
256 devices in a mesh: dp: 32 (over x, z_lo, core), cls: 8 (over y, z_hi).
Axes of the slice: x: 4, y: 4, z: 8 (z_hi: 2, z_lo: 4; z = z_hi * 4 + z_lo), core: 2. Of those that a mesh axis runs over, the one named last changes fastest.
Arguments:
- particles: float32 [2048, 2048], P('dp'), may hold values from -500 to 500
- ctf: float32 [2048, 1024], P('dp'), may hold values from -1 to 1
- references: bfloat16 [32, 2048], P('cls'), may hold values from -0.29882812 to 0.29882812
- noise: float32 [1024], replicated, may hold values from 0.5 to 2
- rotations: int32 [18, 1024], replicated, may hold values from 0 to 1023, each once within a row
- counts: int32 [64], P('dp'), may hold values from 1 to 32, 640 in all
Outputs:
- class_data: float32 [32, 2048], P('cls', 'dp')
- class_weight: float32 [32, 1024], P('cls', 'dp')
- log_evidence: float32 [2048], P('dp')
Inputs may be any that keep to these rules, and one draw needn't show every extreme that they name: `rotations`: each row is a permutation of 0 to 1023. The counts sum to 640; some micrograph has exactly 32 particles.
All inputs are finite; a program needn't handle non-finite values. No bound on the sum of `counts` on one device may be relied on, other than what follows from the above.
Results may differ from a plain program's by a relative error of at most 0.0009.
The roundings to bfloat16 on the way count: a program that leaves them out, or rounds other values in their place, can miss the bound.
Values sent between devices are 32-bit elements; how exact they have to be, the bound alone decides.
A program may use at most 128 MiB of HBM per device.

v0:
```python
import math

import jax
import jax.numpy as jnp
from jax import lax
from jax.sharding import PartitionSpec as P

SIDE = 5
SHIFTS = 25
BLOCK = 32


def phase_tables(coef_count):
    coefs = jnp.arange(coef_count)
    freq_x = (coefs % 32).astype(jnp.float32)
    freq_y = (coefs // 32 - coef_count // 64).astype(jnp.float32)
    offsets = jnp.arange(SHIFTS)
    step_x = (offsets // SIDE - SIDE // 2).astype(jnp.float32)
    step_y = (offsets % SIDE - SIDE // 2).astype(jnp.float32)
    angles = (
        2.0
        * math.pi
        / 64.0
        * (step_x[:, None] * freq_x[None, :] + step_y[:, None] * freq_y[None, :])
    )
    return (jnp.cos(angles), jnp.sin(angles))


def rotate_refs(refs, rotations):
    class_count = refs.shape[0]
    turn_count, coef_count = rotations.shape
    halves = refs.reshape(class_count, 2, coef_count)
    picked = halves[:, :, rotations]
    return jnp.transpose(picked, (0, 2, 1, 3)).reshape(class_count * turn_count, 2 * coef_count)


def inverse_rotations(rotations):
    turn_count, coef_count = rotations.shape
    return (
        jnp.zeros((turn_count, coef_count), jnp.int32)
        .at[jnp.arange(turn_count)[:, None], rotations]
        .set(jnp.arange(coef_count, dtype=jnp.int32)[None, :])
    )


def unrotate(terms, inverse, class_count):
    turn_count, coef_count = inverse.shape
    layered = terms.reshape(class_count, turn_count, -1, coef_count)
    return jnp.sum(jnp.take_along_axis(layered, inverse[None, :, None, :], axis=3), axis=1).reshape(
        class_count, -1
    )


def normalise(scores):
    peak_here = jnp.max(scores, axis=(1, 2))
    peak_score = lax.pmax(peak_here, "cls")
    total_exp = lax.psum(jnp.sum(jnp.exp(scores - peak_score[:, None, None]), axis=(1, 2)), "cls")
    return peak_score + jnp.log(total_exp)


def process(
    rows_x, rows_c, live_rows, block_total, rotated, power, noise, cosine_table, sine_table
):
    coef_count = noise.shape[0]
    capacity = rows_x.shape[0]
    pair_count = rotated.shape[0]
    doubled_noise = jnp.concatenate([noise, noise])[None, :]
    contract_rows = (((0,), (0,)), ((), ()))
    contract_cols = (((1,), (1,)), ((), ()))

    def one_block(block_index, carry):
        evidence_rows, weighted, ctf_weight = carry
        start = block_index * BLOCK
        block_x = lax.dynamic_slice_in_dim(rows_x, start, BLOCK, 0)
        block_c = lax.dynamic_slice_in_dim(rows_c, start, BLOCK, 0)
        valid = start + jnp.arange(BLOCK) < live_rows
        scaled = block_x * jnp.concatenate([block_c, block_c], 1) / doubled_noise
        real_part = scaled[:, None, :coef_count]
        imag_part = scaled[:, None, coef_count:]
        shifted = jnp.concatenate(
            [
                real_part * cosine_table[None] + imag_part * sine_table[None],
                imag_part * cosine_table[None] - real_part * sine_table[None],
            ],
            2,
        )
        shifted = shifted.astype(jnp.bfloat16).reshape(BLOCK * SHIFTS, 2 * coef_count)
        ctf_square = (block_c * block_c).astype(jnp.bfloat16)
        cross = lax.dot_general(
            shifted, rotated, contract_cols, preferred_element_type=jnp.float32
        ).reshape(BLOCK, SHIFTS, pair_count)
        penalty = lax.dot_general(
            ctf_square, power, contract_cols, preferred_element_type=jnp.float32
        )
        scores = cross - 0.5 * penalty[:, None, :]
        evidence = normalise(scores)
        posterior = jnp.where(
            valid[:, None, None], jnp.exp(scores - evidence[:, None, None]), 0.0
        ).astype(jnp.bfloat16)
        weighted = weighted + lax.dot_general(
            posterior.reshape(BLOCK * SHIFTS, pair_count),
            shifted,
            contract_rows,
            preferred_element_type=jnp.float32,
        )
        occupancy = jnp.sum(posterior.astype(jnp.float32), axis=1).astype(jnp.bfloat16)
        ctf_weight = ctf_weight + lax.dot_general(
            occupancy, ctf_square, contract_rows, preferred_element_type=jnp.float32
        )
        evidence_rows = lax.dynamic_update_slice_in_dim(
            evidence_rows, jnp.where(valid, evidence, 0.0), start, 0
        )
        return (evidence_rows, weighted, ctf_weight)

    start_state = (
        jnp.zeros((capacity,), jnp.float32),
        jnp.zeros((pair_count, 2 * coef_count), jnp.float32),
        jnp.zeros((pair_count, coef_count), jnp.float32),
    )
    return lax.fori_loop(0, block_total, one_block, start_state)


def body(particles, ctf, references, noise, rotations, counts):
    coef_count = ctf.shape[1]
    capacity = particles.shape[0]
    class_here = references.shape[0]
    cosine_table, sine_table = phase_tables(coef_count)
    rotated = rotate_refs(references, rotations)
    widened = rotated.astype(jnp.float32)
    power = (
        (
            widened[:, :coef_count] * widened[:, :coef_count]
            + widened[:, coef_count:] * widened[:, coef_count:]
        )
        / noise[None, :]
    ).astype(jnp.bfloat16)
    peer_count = lax.axis_size("dp")
    own_index = lax.axis_index("dp")
    per_peer = capacity // peer_count
    every_count = lax.all_gather(counts, "dp", axis=0, tiled=True)
    loads = jnp.sum(every_count.reshape(peer_count, -1), axis=1)
    heaviest = jnp.sum((loads + peer_count - 1) // peer_count)
    block_total = (heaviest + BLOCK - 1) // BLOCK
    moved_x, moved_c = (
        lax.all_to_all(
            particles.reshape(per_peer, peer_count, 2 * coef_count),
            "dp",
            split_axis=1,
            concat_axis=0,
            tiled=True,
        ),
        lax.all_to_all(
            ctf.reshape(per_peer, peer_count, coef_count),
            "dp",
            split_axis=1,
            concat_axis=0,
            tiled=True,
        ),
    )
    moved_x = moved_x.reshape(capacity, 2 * coef_count)
    moved_c = moved_c.reshape(capacity, coef_count)
    places = jnp.arange(capacity)
    live = places % per_peer * peer_count + own_index < loads[places // per_peer]
    order = jnp.argsort(jnp.where(live, 0, 1).astype(jnp.int32), stable=True)
    live_rows = jnp.sum(live.astype(jnp.int32))
    evidence_rows, weighted, ctf_weight = process(
        moved_x[order],
        moved_c[order],
        live_rows,
        block_total,
        rotated,
        power,
        noise,
        cosine_table,
        sine_table,
    )
    evidence_recv = jnp.zeros((capacity,), jnp.float32).at[order].set(evidence_rows)
    returned = lax.all_to_all(
        evidence_recv.reshape(peer_count, per_peer), "dp", split_axis=0, concat_axis=0, tiled=True
    )
    log_evidence = jnp.transpose(returned).reshape(capacity)
    inverse = inverse_rotations(rotations)
    data_here = unrotate(weighted, inverse, class_here)
    weight_here = unrotate(ctf_weight / noise[None, :], inverse, class_here)
    class_data, class_weight = (
        lax.psum_scatter(data_here, "dp", scatter_dimension=1, tiled=True),
        lax.psum_scatter(weight_here, "dp", scatter_dimension=1, tiled=True),
    )
    return (class_data, class_weight, log_evidence)


def solution(mesh):
    placed = (P("dp", None), P("dp", None), P("cls", None), P(), P(), P("dp"))
    return jax.shard_map(
        body,
        mesh=mesh,
        in_specs=placed,
        out_specs=(P("cls", "dp"), P("cls", "dp"), P("dp")),
        check_vma=False,
    )
```

profile of v0, /device:TPU:1, one launch (start us, length us, event | category | flops | bytes accessed | tf_op | source)
XLA Modules:
  0.0 1036.6 jit_solution(8323793252564454203)
XLA Ops:
  7.2 1.9 copy.27
  9.0 10.0 all-to-all-start.1
  19.1 1.3 dynamic-slice
  21.0 0.9 dynamic-update-slice
  21.9 13.3 %all-reduce = s32[64]{0:T(128)S(1)} all-reduce(s32[64]{0:T(128)S(1)} %dynamic-update-slice), channel_id=1, replica_groups=mesh['dp'=32,'cls'=8] {'dp'}, use_global_device_ids=true, to_apply=%add | all-reduce | flops 64 | bytes 512
  36.8 0.9 fusion.37
  37.7 0.8 and_reduce_fusion
  38.5 0.8 multiply_reduce_fusion
  39.3 67.8 %scatter_custom_fusion.1 = s32[18432]{0:T(1024)S(1)} fusion(s32[18432]{0:T(1024)S(1)} %reshape.265, s32[18432]{0:T(1024)S(1)} %reshape.267, s32[]{:T(128)} %constant.177.clone.1), kind=kCustom, calls=%fused_computation.51 | custom fusion | bytes 73732
  107.2 0.8 gather_fusion
  108.0 0.7 reshape.200
  109.2 2.2 copy.26
  111.5 119.7 %gather_fusion.3 = bf16[18432,4,2]{1,2,0:T(2,128)(2,1)} fusion(bf16[4,2,1024]{0,1,2:T(2,128)(2,1)S(1)} %copy.28, s32[18432]{0:T(1024)S(1)} %broadcast_clamp_fusion), kind=kCustom, calls=%fused_computation.3 | custom fusion | bytes 663552 | tf_op jit(solution)/shard_map/gather | solution.py:33
  231.2 20.5 %copy.29 = bf16[4,18,2,1024]{3,2,1,0:T(2,128)(2,1)S(1)} copy(bf16[4,18,2,1024]{0,2,3,1:T(2,128)(2,1)} %bitcast.74) | data formatting | bytes 589824 | tf_op jit(solution)/shard_map/transpose | solution.py:34
  251.8 0.7 copy-done.1
  252.6 2.0 sort.17
  255.2 7.1 all-to-all-start
  263.4 15.8 %all-to-all-done = f32[2,32,2048]{2,0,1:T(2,128)S(1)} async-done(((f32[2,32,2048]{2,0,1:T(2,128)}), f32[2,32,2048]{2,0,1:T(2,128)S(1)}, u32[]{:S(2)}, u32[]{:S(2)}) %all-to-all-start) | async-done | bytes 524320 | tf_op jit(solution)/shard_map/all_to_all | solution.py:145
  279.6 0.8 gather_fusion.1
  280.4 0.9 broadcast_in_dim.99
  281.3 113.0 %while.19 = (s32[]{:T(128)}, f32[64]{0:T(128)S(1)}, f32[72,2048]{1,0:T(8,128)}, f32[72,1024]{1,0:T(8,128)S(1)}, s32[]{:T(128)}, /*index=5*/s32[]{:T(128)}, f32[6...) while((s32[]{:T(128)}, f32[64]{0:T(128)S(1)}, ...), condition=%wide.region_11.12_spmd.clone.clone.clone, body=%wide.region_5.11_spmd.clone.clone.clone.sunk | while | flops 502069376 | bytes 21940116 | solution.py:120
  282.1 1.0 add_convert_fusion.2
  283.1 1.2 copy-done
  284.3 2.1 fusion.60
  286.4 27.0 %pmax.14 = f32[32]{0:T(128)S(1)} all-reduce(f32[32]{0:T(128)S(1)} %get-tuple-element.468), channel_id=1, replica_groups=mesh['dp'=32,'cls'=8] {'cls'}, use_global_device_ids=true, to_apply=%region_7.7 | all-reduce | flops 32 | bytes 256 | tf_op jit(solution)/shard_map/while/body/pmax | solution.py:56
  313.7 20.4 %psum.14 = f32[32]{0:T(128)S(1)} all-reduce(f32[32]{0:T(128)S(1)} %exponential_reduce_fusion.2), channel_id=1, replica_groups=mesh['dp'=32,'cls'=8] {'cls'}, use_global_device_ids=true, to_apply=%region_9.9 | all-reduce | flops 32 | bytes 256 | tf_op jit(solution)/shard_map/while/body/psum | solution.py:57
  334.1 0.7 select_dynamic-update-slice_fusion.2
  335.0 3.2 fusion.62
  339.3 1.0 add_convert_fusion.2
  340.3 1.2 copy-done
  341.5 2.1 fusion.60
  343.6 25.7 %pmax.14 = f32[32]{0:T(128)S(1)} all-reduce(f32[32]{0:T(128)S(1)} %get-tuple-element.468), channel_id=1, replica_groups=mesh['dp'=32,'cls'=8] {'cls'}, use_global_device_ids=true, to_apply=%region_7.7 | all-reduce | flops 32 | bytes 256 | tf_op jit(solution)/shard_map/while/body/pmax | solution.py:56
  369.5 20.4 %psum.14 = f32[32]{0:T(128)S(1)} all-reduce(f32[32]{0:T(128)S(1)} %exponential_reduce_fusion.2), channel_id=1, replica_groups=mesh['dp'=32,'cls'=8] {'cls'}, use_global_device_ids=true, to_apply=%region_9.9 | all-reduce | flops 32 | bytes 256 | tf_op jit(solution)/shard_map/while/body/psum | solution.py:57
  389.9 0.7 select_dynamic-update-slice_fusion.2
  390.8 3.2 fusion.62
  394.3 1.6 reshape.202
  395.9 5.1 copy.32
  401.0 266.0 %gather_fusion.5 = f32[18432,4]{1,0:T(8,128)} fusion(f32[4,18,1024]{0,2,1:T(8,128)} %copy.32, s32[18432]{0:T(1024)S(1)} %reshape.243), kind=kCustom, calls=%fused_computation.5 | custom fusion | bytes 737280 | tf_op jit(solution)/shard_map/jit(take_along_axis)/gather | solution.py:49
  667.0 10.0 select_reduce_fusion
  677.1 17.9 %copy.30 = f32[4,18,2,1024]{0,2,3,1:T(2,128)} copy(f32[4,18,2,1024]{3,2,1,0:T(2,128)S(1)} %reshape.202) | data formatting | bytes 1179648 | tf_op jit(solution)/shard_map/reshape | solution.py:48
  695.0 162.1 %gather_fusion.4 = f32[18432,4,2]{1,2,0:T(2,128)} fusion(f32[4,18,2,1024]{0,2,3,1:T(2,128)} %copy.30, s32[18432]{0:T(1024)S(1)} %reshape.243), kind=kCustom, calls=%fused_computation.4 | custom fusion | bytes 1327104 | tf_op jit(solution)/shard_map/jit(take_along_axis)/gather | solution.py:49
  857.1 18.7 %copy.36 = f32[18,1024,4,2]{1,0,3,2:T(8,128)S(1)} copy(f32[18,1024,4,2]{2,3,1,0:T(2,128)} %bitcast.72) | data formatting | bytes 1179648 | tf_op jit(solution)/shard_map/jit(take_along_axis)/gather | solution.py:49
  875.9 1.4 copy.41
  877.3 0.8 scatter_custom_fusion
  878.2 25.4 %all_to_all.42 = f32[32,1,2]{2,1,0:T(1,128)S(1)} all-to-all(f32[32,1,2]{2,1,0:T(1,128)S(1)} %bitcast.87), channel_id=1, replica_groups=mesh['dp'=32,'cls'=8] {'dp'}, dimensions={0} | all-to-all | bytes 512 | tf_op jit(solution)/shard_map/all_to_all | solution.py:178
  904.3 1.4 copy.40
  905.7 122.7 %reduce-scatter.7.cloned.1.call-done = f32[64,4]{1,0:T(8,128)} async-done(((f32[2048,4]{1,0:T(8,128)}), f32[64,4]{1,0:T(8,128)}) %reduce-scatter.7.cloned.1.call-update) | async-done | bytes 1040
  1028.3 1.4 copy.38
  (67 shorter events, 7.6 us)
Async XLA Ops:
  7.2 255.2 %copy-start.2 = (f32[1024]{0:T(1024)S(1)}, f32[1024]{0:T(1024)}, u32[]{:S(2)}) copy-start(f32[1024]{0:T(1024)} %param.11) | copy-start | bytes 12292
  9.0 246.2 %all-to-all-start.1 = ((f32[2,32,1024]{2,0,1:T(2,128)}), f32[2,32,1024]{2,0,1:T(2,128)S(1)}, u32[]{:S(2)}, u32[]{:S(2)}) async-start(f32[2,32,1024]{2,0,1:T(2,128)} %copy.27), calls=%async_computation.1 | async-start | bytes 524288 | tf_op jit(solution)/shard_map/all_to_all | solution.py:152
  251.8 0.7 copy-start.1
  255.2 24.0 %all-to-all-start = ((f32[2,32,2048]{2,0,1:T(2,128)}), f32[2,32,2048]{2,0,1:T(2,128)S(1)}, u32[]{:S(2)}, u32[]{:S(2)}) async-start(f32[2,32,2048]{2,0,1:T(2,128)} %copy.26), calls=%async_computation | async-start | bytes 1048576 | tf_op jit(solution)/shard_map/all_to_all | solution.py:145
  262.3 642.0 %reduce-scatter.9.cloned.1.call-start = ((), (), s32[]{:S(2)}) async-start(), calls=%async_computation.6 | async-start | bytes 540672
  283.1 1.2 copy-start
  340.3 1.2 copy-start
  677.0 351.3 %reduce-scatter.7.cloned.1.call-start = ((), (), s32[]{:S(2)}) async-start(), calls=%async_computation.5 | async-start | bytes 1081344
Sparse Core Ops, SparseCore 0:
  677.2 150.0 reduce-scatter.8
  877.5 150.8 reduce-scatter.6
where the time goes:
time: 1040 us
  local copies, waits for them, and re-layouts  700 us (67%)
  waiting for transfers between devices  139 us (13%)
  blocking collectives  132 us (13%)
  other arithmetic  21.9 us (2%)
  starting transfers between devices  17.2 us (2%)
  between operations  15.7 us (2%)
  matrix products  11.2 us (1%)
    gather x4, local copies, waits for them, and re-layouts, unrotate(): jnp.take_along_axis(layered, inverse[None, :, None, :], axis=3)  447 us
    unnamed x4, waiting for transfers between devices  123 us
    gather x1, local copies, waits for them, and re-layouts, rotate_refs(): picked = halves[:, :, rotations]  120 us
    unnamed x13, local copies, waits for them, and re-layouts  74.9 us
    pmax x2, blocking collectives, normalise(): peak_score = lax.pmax(peak_here, 'cls')  52.7 us
    psum x2, blocking collectives, normalise(): lax.psum(jnp.sum(jnp.exp(scores - peak_score[:, None, None]), axis=(1, 2)...  40.8 us
    all_to_all x1, blocking collectives, body(): lax.all_to_all(evidence_recv.reshape(peer_count, per_peer), 'dp', split_a...  25.4 us
    reshape x4, local copies, waits for them, and re-layouts, unrotate(): layered = terms.reshape(class_count, turn_count, -1, coef_count)  24.6 us
  transfers between devices with their start and end apart: 4, of which 2 were waited for; matrix products, arithmetic and copies ran while one was open for 41% of the time, Pallas kernels for 0%

commit v1 on v0

v1 whole, which is shorter than its diff:
```python
import functools
import math

import jax
import jax.numpy as jnp
import numpy as np
from jax import lax
from jax.experimental import pallas as pl
from jax.experimental.pallas import tpu as pltpu
from jax.sharding import PartitionSpec as P

SIDE = 5
SHIFTS = 25
LANES = 128
TURNS = 18
QPAD = 80
MESH = pl.DeviceIdType.MESH


def phase_tables(coef_count, rows):
    coefs = np.arange(coef_count)
    freq_x = (coefs % 32).astype(np.float32)
    freq_y = (coefs // 32 - coef_count // 64).astype(np.float32)
    offsets = np.arange(SHIFTS)
    step_x = (offsets // SIDE - SIDE // 2).astype(np.float32)
    step_y = (offsets % SIDE - SIDE // 2).astype(np.float32)
    angles = np.float32(2.0 * math.pi / 64.0) * (
        step_x[:, None] * freq_x[None, :] + step_y[:, None] * freq_y[None, :]
    )
    wide = angles.astype(np.float32).astype(np.float64)
    pad = ((0, rows - SHIFTS), (0, 0))
    return (
        np.pad(np.cos(wide).astype(np.float32), pad),
        np.pad(np.sin(wide).astype(np.float32), pad),
    )


def iota(shape, axis):
    return lax.broadcasted_iota(jnp.int32, shape, axis)


def lane_take(values, index):
    return jnp.take_along_axis(values, index, axis=1, mode="promise_in_bounds")


def kernel(
    dims,
    counts_ref,
    part_ref,
    ctf_ref,
    refs_ref,
    noise_ref,
    rot_ref,
    cos_ref,
    sin_ref,
    data_ref,
    weight_ref,
    evid_ref,
    scaled,
    csq,
    shifted,
    rotated,
    scores,
    weighted,
    inverse,
    turns,
    total,
    stat_send,
    stat_recv,
    piece_send,
    piece_recv,
    stat_sems,
    piece_sems,
):
    n_dp, n_cls, slots, coefs = dims
    tiles = coefs // LANES
    pairs = TURNS // 2
    shift_rows = shifted.shape[0]
    lanes_used = SHIFTS * slots
    me_dp = lax.axis_index("dp")
    me_cls = lax.axis_index("cls")

    barrier = pltpu.get_barrier_semaphore()

    def greet_dp(o, c):
        pl.semaphore_signal(
            barrier, inc=1, device_id=(lax.rem(me_dp + o, n_dp), me_cls), device_id_type=MESH
        )
        return c

    def greet_cls(o, c):
        pl.semaphore_signal(
            barrier, inc=1, device_id=(me_dp, lax.rem(me_cls + o, n_cls)), device_id_type=MESH
        )
        return c

    lax.fori_loop(1, n_dp, greet_dp, 0)
    lax.fori_loop(1, n_cls, greet_cls, 0)

    noise = noise_ref[...]
    transfer = ctf_ref[...]
    scaled[:, :coefs] = part_ref[:, :coefs] * transfer / noise
    scaled[:, coefs:] = part_ref[:, coefs:] * transfer / noise
    csq[...] = (transfer * transfer).astype(jnp.bfloat16)

    def one_shift(s, c):
        cosine = cos_ref[pl.ds(s, 1), :]
        sine = sin_ref[pl.ds(s, 1), :]
        rows = pl.ds(pl.multiple_of(s * slots, slots), slots)
        real = scaled[:, :coefs]
        imag = scaled[:, coefs:]
        shifted[rows, :coefs] = (real * cosine + imag * sine).astype(jnp.bfloat16)
        shifted[rows, coefs:] = (imag * cosine - real * sine).astype(jnp.bfloat16)
        return c

    lax.fori_loop(0, shift_rows // slots, one_shift, 0)

    low_half = iota((8, LANES), 0) < 4
    for r in range(TURNS):
        turns[r] = jnp.broadcast_to(rot_ref[r : r + 1, :], (8, coefs))
    refs4 = refs_ref[...].astype(jnp.float32)
    total[:, : 2 * coefs] = jnp.concatenate([refs4, refs4], axis=0)

    def rotate_pair(p, c):
        rows = pl.ds(pl.multiple_of(p * 8, 8), 8)
        for j in range(tiles):
            cols = slice(j * LANES, (j + 1) * LANES)
            index = jnp.where(low_half, turns[2 * p, :, cols], turns[2 * p + 1, :, cols])
            lane = index & (LANES - 1)
            tile = lax.shift_right_logical(index, 7)
            for part in range(2):
                found = jnp.zeros((8, LANES), jnp.float32)
                for s in range(tiles):
                    base = part * coefs + s * LANES
                    picked = lane_take(total[:, base : base + LANES], lane)
                    found = jnp.where(tile == s, picked, found)
                base = part * coefs + j * LANES
                rotated[rows, base : base + LANES] = found
        return c

    lax.fori_loop(0, pairs, rotate_pair, 0)
    rot_rows = rotated.shape[0]
    turned = rotated[...]
    power = (
        (turned[:, :coefs] * turned[:, :coefs] + turned[:, coefs:] * turned[:, coefs:]) / noise
    ).astype(jnp.bfloat16)
    pad_rows = jnp.zeros((QPAD - rot_rows, 2 * coefs), jnp.float32)
    turned = jnp.concatenate([turned, pad_rows], axis=0).astype(jnp.bfloat16)
    squares = csq[...]
    contract_cols = (((1,), (1,)), ((), ()))
    penalty = lax.dot_general(
        power,
        jnp.concatenate([squares, squares], axis=0),
        contract_cols,
        preferred_element_type=jnp.float32,
    )
    half_penalty = 0.5 * penalty

    lane_row = iota((1, LANES), 1)
    peak = jnp.full((1, LANES), -jnp.inf, jnp.float32)
    chunks = shift_rows // LANES
    for j in range(chunks):
        block = shifted[j * LANES : (j + 1) * LANES, :]
        cross = lax.dot_general(
            turned, block, contract_cols, preferred_element_type=jnp.float32
        )[:rot_rows]
        values = cross - half_penalty
        if (j + 1) * LANES > lanes_used:
            values = jnp.where(j * LANES + lane_row < lanes_used, values, -1e30)
        scores[:, j * LANES : (j + 1) * LANES] = values
        peak = jnp.maximum(peak, jnp.max(values, axis=0, keepdims=True))
    peak = jnp.maximum(peak, pltpu.roll(peak, slots, 1))
    mass = jnp.zeros((1, LANES), jnp.float32)
    for j in range(chunks):
        cols = slice(j * LANES, (j + 1) * LANES)
        values = jnp.exp(scores[:, cols] - peak)
        if (j + 1) * LANES > lanes_used:
            values = jnp.where(j * LANES + lane_row < lanes_used, values, 0.0)
        scores[:, cols] = values
        mass = mass + jnp.sum(values, axis=0, keepdims=True)
    mass = mass + pltpu.roll(mass, slots, 1)
    stat_send[...] = jnp.where(iota((8, LANES), 0) == 0, peak, mass)

    pl.semaphore_wait(barrier, n_dp - 1 + n_cls - 1)

    def stat_copy(o):
        return pltpu.make_async_remote_copy(
            src_ref=stat_send,
            dst_ref=stat_recv.at[o - 1],
            send_sem=stat_sems.at[0],
            recv_sem=stat_sems.at[1],
            device_id=(me_dp, lax.rem(me_cls + o, n_cls)),
            device_id_type=MESH,
        )

    def stat_start(o, c):
        stat_copy(o).start()
        return c

    lax.fori_loop(1, n_cls, stat_start, 0)

    place = iota((1, coefs), 1)
    place_low = (place & (LANES - 1)).astype(jnp.float32)
    place_high = lax.shift_right_logical(place, 7).astype(jnp.float32)

    def invert(r, c):
        row = turns[r, 0:1, :]
        lane = row & (LANES - 1)
        tile = lax.shift_right_logical(row, 7)
        hot = jnp.where(iota((LANES, coefs), 0) == lane, 1.0, 0.0).astype(jnp.bfloat16)
        mine = iota((tiles, coefs), 0) == tile
        source = jnp.concatenate(
            [jnp.where(mine, place_low, 0.0), jnp.where(mine, place_high, 0.0)], axis=0
        ).astype(jnp.bfloat16)
        inverse[r] = lax.dot_general(
            source, hot, contract_cols, preferred_element_type=jnp.float32
        ).astype(jnp.int32)
        return c

    lax.fori_loop(0, TURNS, invert, 0)

    pltpu.make_async_copy(stat_recv, stat_recv, stat_sems.at[1]).wait()
    pltpu.make_async_copy(stat_recv, stat_recv, stat_sems.at[0]).wait()

    top = peak
    for o in range(n_cls - 1):
        top = jnp.maximum(top, stat_recv[o, 0:1, :])
    sums = mass * jnp.exp(peak - top)
    for o in range(n_cls - 1):
        sums = sums + stat_recv[o, 1:2, :] * jnp.exp(stat_recv[o, 0:1, :] - top)
    evidence = top + jnp.log(sums)
    live = (lane_row & (slots - 1)) < counts_ref[0] + counts_ref[1]
    factor = jnp.where(live, jnp.exp(peak - evidence), 0.0)
    evid_ref[...] = jnp.where(live, evidence, 0.0)[:, :slots]

    occupancy = jnp.zeros((rot_rows, LANES), jnp.float32)
    posterior = []
    for j in range(chunks):
        cols = slice(j * LANES, (j + 1) * LANES)
        values = (scores[:, cols] * factor).astype(jnp.bfloat16).astype(jnp.float32)
        occupancy = occupancy + values
        posterior.append(
            jnp.concatenate(
                [values, jnp.zeros((QPAD - rot_rows, LANES), jnp.float32)], axis=0
            ).astype(jnp.bfloat16)
        )
    posterior = jnp.concatenate(posterior, axis=1)
    weighted[:, : 2 * coefs] = lax.dot_general(
        posterior,
        shifted[...],
        (((1,), (0,)), ((), ())),
        preferred_element_type=jnp.float32,
    )[:rot_rows]
    occupancy = occupancy + pltpu.roll(occupancy, slots, 1)
    occupancy = jnp.where(lane_row < slots, occupancy, 0.0)
    occupancy = jnp.concatenate(
        [occupancy, jnp.zeros((QPAD - rot_rows, LANES), jnp.float32)], axis=0
    ).astype(jnp.bfloat16)
    weighted[:, 2 * coefs :] = (
        lax.dot_general(
            occupancy,
            jnp.concatenate([squares, squares], axis=0),
            (((1,), (0,)), ((), ())),
            preferred_element_type=jnp.float32,
        )[:rot_rows]
        / noise
    )

    total[...] = jnp.zeros_like(total)

    def unrotate_pair(p, c):
        rows = pl.ds(pl.multiple_of(p * 8, 8), 8)
        for j in range(tiles):
            lane = jnp.where(
                low_half, inverse[2 * p, j : j + 1, :], inverse[2 * p + 1, j : j + 1, :]
            )
            tile = jnp.where(
                low_half,
                inverse[2 * p, tiles + j : tiles + j + 1, :],
                inverse[2 * p + 1, tiles + j : tiles + j + 1, :],
            )
            for part in range(3):
                found = jnp.zeros((8, LANES), jnp.float32)
                for s in range(tiles):
                    base = part * coefs + s * LANES
                    picked = lane_take(weighted[rows, base : base + LANES], lane)
                    found = jnp.where(tile == s, picked, found)
                base = part * coefs + j * LANES
                total[:, base : base + LANES] += found
        return c

    lax.fori_loop(0, pairs, unrotate_pair, 0)

    n_pieces = n_dp // 2
    for e in range(n_pieces):
        data = total[:, e * LANES : (e + 1) * LANES]
        base = 2 * coefs + (e // 2) * LANES
        mass_tile = total[:, base : base + LANES]
        data = data + pltpu.roll(data, 4, 0)
        mass_tile = mass_tile + pltpu.roll(mass_tile, 4, 0)
        piece_send[e] = jnp.where(low_half, data, mass_tile)

    def piece_start(o, c):
        target = lax.rem(me_dp + o, n_dp)
        pltpu.make_async_remote_copy(
            src_ref=piece_send.at[lax.div(target, 2)],
            dst_ref=piece_recv.at[o - 1],
            send_sem=piece_sems.at[0],
            recv_sem=piece_sems.at[1],
            device_id=(target, me_cls),
            device_id_type=MESH,
        ).start()
        return c

    lax.fori_loop(1, n_dp, piece_start, 0)
    pltpu.make_async_copy(piece_recv, piece_recv, piece_sems.at[1]).wait()
    gathered = piece_send[lax.div(me_dp, 2)]
    for o in range(n_dp - 1):
        gathered = gathered + piece_recv[o]
    data_part = lax.rem(me_dp, 2)
    weight_part = lax.rem(me_dp, 4)
    data_out = jnp.where(data_part == 0, gathered, pltpu.roll(gathered, 64, 1))
    data_ref[...] = data_out[0:4, :64]
    weight_out = gathered
    for w in range(1, 4):
        weight_out = jnp.where(weight_part == w, pltpu.roll(gathered, LANES - 32 * w, 1), weight_out)
    weight_ref[...] = weight_out[4:8, :32]
    pltpu.make_async_copy(piece_recv, piece_recv, piece_sems.at[0]).wait()


def body(particles, ctf, references, noise, rotations, counts):
    slots, coefs = ctf.shape
    classes = references.shape[0]
    n_dp = lax.axis_size("dp")
    n_cls = lax.axis_size("cls")
    padded = SHIFTS + 1
    cosine, sine = phase_tables(coefs, padded)
    rows = padded * slots
    pair_count = classes * TURNS
    vmem = pl.BlockSpec(memory_space=pltpu.VMEM)
    data, weight, evidence = pl.pallas_call(
        functools.partial(kernel, (n_dp, n_cls, slots, coefs)),
        out_shape=(
            jax.ShapeDtypeStruct((classes, 2 * coefs // n_dp), jnp.float32),
            jax.ShapeDtypeStruct((classes, coefs // n_dp), jnp.float32),
            jax.ShapeDtypeStruct((1, slots), jnp.float32),
        ),
        in_specs=[pl.BlockSpec(memory_space=pltpu.SMEM)] + [vmem] * 7,
        out_specs=(vmem, vmem, vmem),
        scratch_shapes=[
            pltpu.VMEM((slots, 2 * coefs), jnp.float32),
            pltpu.VMEM((slots, coefs), jnp.bfloat16),
            pltpu.VMEM((rows, 2 * coefs), jnp.bfloat16),
            pltpu.VMEM((pair_count, 2 * coefs), jnp.float32),
            pltpu.VMEM((pair_count, rows), jnp.float32),
            pltpu.VMEM((pair_count, 3 * coefs), jnp.float32),
            pltpu.VMEM((TURNS, 2 * coefs // LANES, LANES), jnp.int32),
            pltpu.VMEM((TURNS, 8, coefs), jnp.int32),
            pltpu.VMEM((8, 3 * coefs), jnp.float32),
            pltpu.VMEM((8, LANES), jnp.float32),
            pltpu.VMEM((n_cls - 1, 8, LANES), jnp.float32),
            pltpu.VMEM((n_dp // 2, 8, LANES), jnp.float32),
            pltpu.VMEM((n_dp - 1, 8, LANES), jnp.float32),
            pltpu.SemaphoreType.DMA((2,)),
            pltpu.SemaphoreType.DMA((2,)),
        ],
        compiler_params=pltpu.CompilerParams(
            collective_id=0, has_side_effects=True, vmem_limit_bytes=48 << 20
        ),
        name="class_average",
    )(
        counts,
        particles,
        ctf,
        references,
        noise.reshape(1, coefs),
        rotations,
        jnp.asarray(cosine),
        jnp.asarray(sine),
    )
    return data, weight, evidence.reshape(slots)


def solution(mesh):
    placed = (P("dp", None), P("dp", None), P("cls", None), P(), P(), P("dp"))
    return jax.shard_map(
        body,
        mesh=mesh,
        in_specs=placed,
        out_specs=(P("cls", "dp"), P("cls", "dp"), P("dp")),
        check_vma=False,
    )
```

time: 1040 us -> 40.4 us (0.04)
  local copies, waits for them, and re-layouts: 700 us -> 8.41 us
  waiting for transfers between devices: 139 us -> 0 us
  blocking collectives: 132 us -> 0 us
  Pallas kernels: 0 us -> 31 us
  other arithmetic: 21.9 us -> 0 us
  starting transfers between devices: 17.2 us -> 0 us
  between operations: 15.7 us -> 0.66 us
  matrix products: 11.2 us -> 0 us
    gather x8 -> x0, local copies, waits for them, and re-layouts: 569 us -> none  [the longest x4 447 us: unrotate(): jnp.take_along_axis(layered, inverse[None, :, None, :], axis=3)]
    unnamed x4 -> x0, waiting for transfers between devices: 123 us -> none
    unnamed x13 -> x19, local copies, waits for them, and re-layouts: 74.9 us -> 8.41 us
    pmax x2 -> x0, blocking collectives: 52.7 us -> none  [normalise(): peak_score = lax.pmax(peak_here, 'cls')]
    psum x2 -> x0, blocking collectives: 40.8 us -> none  [normalise(): lax.psum(jnp.sum(jnp.exp(scores - peak_score[:, None, None]), axis=(1, 2)...]
    reshape x12 -> x0, local copies, waits for them, and re-layouts: 31.2 us -> none  [the longest x4 24.6 us: unrotate(): layered = terms.reshape(class_count, turn_count, -1, coef_count)]
    pallas_call x0 -> x1, Pallas kernels: none -> 31 us  [body(): pl.pallas_call(functools.partial(kernel, (n_dp, n_cls, slots, coefs)), ou...]
    all_to_all x1 -> x0, blocking collectives: 25.4 us -> none  [body(): lax.all_to_all(evidence_recv.reshape(peer_count, per_peer), 'dp', split_a...]
  transfers between devices with their start and end apart: 4 -> 0, of which waited for: 2 -> 0; matrix products, arithmetic and copies ran while one was open for 41% -> 0% of each run, Pallas kernels for 0% -> 0%
where the time goes in v1:
time: 40.4 us; the launch traced here: 40 us
  Pallas kernels  31 us (77%)
  local copies, waits for them, and re-layouts  8.41 us (21%)
  between operations  0.66 us (2%)
    pallas_call x1, Pallas kernels, body(): pl.pallas_call(functools.partial(kernel, (n_dp, n_cls, slots, coefs)), ou...  31 us
    unnamed x19, local copies, waits for them, and re-layouts  8.41 us

profile of v1, /device:TPU:1, one launch (start us, length us, event | category | flops | bytes accessed | tf_op | source)
XLA Modules:
  0.0 40.0 jit_solution(1776666390447804462)
XLA Ops:
  0.6 0.0 copy-start.7
  0.6 0.6 %copy-done.7 = s32[2]{0:T(128)S(1)} copy-done((s32[2]{0:T(128)S(1)}, s32[2]{0:T(128)}, u32[]{:S(2)}) %copy-start.7) | copy-done | bytes 32
  1.3 0.0 copy-start
  1.3 1.0 %copy-done = f32[64,2048]{1,0:T(8,128)S(1)} copy-done((f32[64,2048]{1,0:T(8,128)S(1)}, f32[64,2048]{1,0:T(8,128)}, u32[]{:S(2)}) %copy-start) | copy-done | bytes 524312
  2.3 0.0 copy-start.1
  2.3 0.9 %copy-done.1 = f32[64,1024]{1,0:T(8,128)S(1)} copy-done((f32[64,1024]{1,0:T(8,128)S(1)}, f32[64,1024]{1,0:T(8,128)}, u32[]{:S(2)}) %copy-start.1) | copy-done | bytes 262168
  3.3 0.0 copy-start.2
  3.3 0.9 %copy-done.2 = f32[26,1024]{1,0:T(8,128)S(1)} copy-done((f32[26,1024]{1,0:T(8,128)S(1)}, f32[26,1024]{1,0:T(8,128)}, u32[]{:S(2)}) %copy-start.2) | copy-done | bytes 106520
  4.2 0.0 copy-start.3
  4.2 0.9 %copy-done.3 = f32[26,1024]{1,0:T(8,128)S(1)} copy-done((f32[26,1024]{1,0:T(8,128)S(1)}, f32[26,1024]{1,0:T(8,128)}, u32[]{:S(2)}) %copy-start.3) | copy-done | bytes 106520
  5.1 0.0 copy-start.4
  5.1 0.9 %copy-done.4 = s32[18,1024]{1,0:T(8,128)S(1)} copy-done((s32[18,1024]{1,0:T(8,128)S(1)}, s32[18,1024]{1,0:T(8,128)}, u32[]{:S(2)}) %copy-start.4) | copy-done | bytes 73752
  6.0 0.0 copy-start.5
  6.0 0.7 %copy-done.5 = bf16[4,2048]{1,0:T(4,128)(2,1)S(1)} copy-done((bf16[4,2048]{1,0:T(4,128)(2,1)S(1)}, bf16[4,2048]{1,0:T(4,128)(2,1)}, u32[]{:S(2)}) %copy-start.5) | copy-done | bytes 16408
  6.7 0.0 copy-start.6
  6.7 0.7 %copy-done.6 = f32[1024]{0:T(1024)S(1)} copy-done((f32[1024]{0:T(1024)S(1)}, f32[1024]{0:T(1024)}, u32[]{:S(2)}) %copy-start.6) | copy-done | bytes 4120
  7.4 31.0 %class_average.1 = (f32[4,64]{1,0:T(4,128)S(1)}, f32[4,32]{1,0:T(4,128)S(1)}, f32[1,64]{1,0:T(1,128)S(1)}) custom-call(s32[2]{0:T(128)S(1)} %copy-done.7, f32[64,2048]{1,0:T(8,128)S(1)} %copy-done, f32[64,1024]{1,0:T(8,128)S(1)} %copy-done.1, bf16[4,2048]{1,0:T(4,128)(2,1)S(1)} %copy-done.5, f32[1,1024]{1,0:T(1,128)S(1)} %bitcast.2, ...), custom_call_target="tpu_custom_call" | custom-call | tf_op jit(solution)/shard_map/class_average/pallas_call | solution.py:341
  38.4 0.6 %copy.14 = f32[4,64]{1,0:T(4,128)} copy(f32[4,64]{1,0:T(4,128)S(1)} %get-tuple-element.12) | data formatting | bytes 2048
  38.9 0.6 %copy.15 = f32[4,32]{1,0:T(4,128)} copy(f32[4,32]{1,0:T(4,128)S(1)} %get-tuple-element.13) | data formatting | bytes 1024
  39.5 0.5 %copy.16 = f32[64]{0:T(128)} copy(f32[64]{0:T(128)S(1)} %bitcast.3) | data formatting | bytes 512
Async XLA Ops:
  0.6 0.7 %copy-start.7 = (s32[2]{0:T(128)S(1)}, s32[2]{0:T(128)}, u32[]{:S(2)}) copy-start(s32[2]{0:T(128)} %counts_ref.1) | copy-start | bytes 28
  1.3 1.0 %copy-start = (f32[64,2048]{1,0:T(8,128)S(1)}, f32[64,2048]{1,0:T(8,128)}, u32[]{:S(2)}) copy-start(f32[64,2048]{1,0:T(8,128)} %part_ref.1) | copy-start | bytes 1572868
  2.3 0.9 %copy-start.1 = (f32[64,1024]{1,0:T(8,128)S(1)}, f32[64,1024]{1,0:T(8,128)}, u32[]{:S(2)}) copy-start(f32[64,1024]{1,0:T(8,128)} %ctf_ref.1) | copy-start | bytes 786436
  3.3 0.9 %copy-start.2 = (f32[26,1024]{1,0:T(8,128)S(1)}, f32[26,1024]{1,0:T(8,128)}, u32[]{:S(2)}) copy-start(f32[26,1024]{1,0:T(8,128)} %constant.5.clone.sin_ref) | copy-start | bytes 319492
  4.2 0.9 %copy-start.3 = (f32[26,1024]{1,0:T(8,128)S(1)}, f32[26,1024]{1,0:T(8,128)}, u32[]{:S(2)}) copy-start(f32[26,1024]{1,0:T(8,128)} %constant.4.clone.cos_ref) | copy-start | bytes 319492
  5.1 0.9 %copy-start.4 = (s32[18,1024]{1,0:T(8,128)S(1)}, s32[18,1024]{1,0:T(8,128)}, u32[]{:S(2)}) copy-start(s32[18,1024]{1,0:T(8,128)} %rot_ref.1) | copy-start | bytes 221188
  6.0 0.7 %copy-start.5 = (bf16[4,2048]{1,0:T(4,128)(2,1)S(1)}, bf16[4,2048]{1,0:T(4,128)(2,1)}, u32[]{:S(2)}) copy-start(bf16[4,2048]{1,0:T(4,128)(2,1)} %refs_ref.1) | copy-start | bytes 49156
  6.7 0.7 %copy-start.6 = (f32[1024]{0:T(1024)S(1)}, f32[1024]{0:T(1024)}, u32[]{:S(2)}) copy-start(f32[1024]{0:T(1024)} %param.11) | copy-start | bytes 12292

commit v2 on v1

--- a/solution.py
+++ b/solution.py
@@ -45,17 +45,23 @@
 
 def kernel(
     dims,
+    counts_hbm,
+    part_hbm,
+    ctf_hbm,
+    refs_hbm,
+    noise_hbm,
+    rot_hbm,
+    trig_hbm,
+    data_ref,
+    weight_ref,
+    evid_ref,
     counts_ref,
     part_ref,
     ctf_ref,
     refs_ref,
     noise_ref,
     rot_ref,
-    cos_ref,
-    sin_ref,
-    data_ref,
-    weight_ref,
-    evid_ref,
+    trig_ref,
     scaled,
     csq,
     shifted,
@@ -67,8 +73,10 @@
     total,
     stat_send,
     stat_recv,
+    piece_weight,
     piece_send,
     piece_recv,
+    load_sems,
     stat_sems,
     piece_sems,
 ):
@@ -80,6 +88,23 @@
     me_dp = lax.axis_index("dp")
     me_cls = lax.axis_index("cls")
 
+    loads = [
+        pltpu.make_async_copy(source, target, load_sems.at[i])
+        for i, (source, target) in enumerate(
+            (
+                (rot_hbm, rot_ref),
+                (refs_hbm, refs_ref),
+                (noise_hbm, noise_ref),
+                (part_hbm, part_ref),
+                (ctf_hbm, ctf_ref),
+                (trig_hbm, trig_ref),
+                (counts_hbm, counts_ref),
+            )
+        )
+    ]
+    for load in loads:
+        load.start()
+
     barrier = pltpu.get_barrier_semaphore()
 
     def greet_dp(o, c):
@@ -96,6 +121,9 @@
 
     lax.fori_loop(1, n_dp, greet_dp, 0)
     lax.fori_loop(1, n_cls, greet_cls, 0)
+
+    for load in loads:
+        load.wait()
 
     noise = noise_ref[...]
     transfer = ctf_ref[...]
@@ -104,8 +132,8 @@
     csq[...] = (transfer * transfer).astype(jnp.bfloat16)
 
     def one_shift(s, c):
-        cosine = cos_ref[pl.ds(s, 1), :]
-        sine = sin_ref[pl.ds(s, 1), :]
+        cosine = trig_ref[s, 0:1, :]
+        sine = trig_ref[s, 1:2, :]
         rows = pl.ds(pl.multiple_of(s * slots, slots), slots)
         real = scaled[:, :coefs]
         imag = scaled[:, coefs:]
@@ -119,7 +147,7 @@
     for r in range(TURNS):
         turns[r] = jnp.broadcast_to(rot_ref[r : r + 1, :], (8, coefs))
     refs4 = refs_ref[...].astype(jnp.float32)
-    total[:, : 2 * coefs] = jnp.concatenate([refs4, refs4], axis=0)
+    total[...] = jnp.concatenate([refs4, refs4], axis=0)
 
     def rotate_pair(p, c):
         rows = pl.ds(pl.multiple_of(p * 8, 8), 8)
@@ -203,7 +231,7 @@
     place_low = (place & (LANES - 1)).astype(jnp.float32)
     place_high = lax.shift_right_logical(place, 7).astype(jnp.float32)
 
-    def invert(r, c):
+    def invert(r):
         row = turns[r, 0:1, :]
         lane = row & (LANES - 1)
         tile = lax.shift_right_logical(row, 7)
@@ -212,12 +240,18 @@
         source = jnp.concatenate(
             [jnp.where(mine, place_low, 0.0), jnp.where(mine, place_high, 0.0)], axis=0
         ).astype(jnp.bfloat16)
-        inverse[r] = lax.dot_general(
+        return lax.dot_general(
             source, hot, contract_cols, preferred_element_type=jnp.float32
         ).astype(jnp.int32)
-        return c
-
-    lax.fori_loop(0, TURNS, invert, 0)
+
+    def invert_pair(p, c):
+        first = invert(2 * p)
+        second = invert(2 * p + 1)
+        for j in range(2 * tiles):
+            inverse[p, j] = jnp.where(low_half, first[j : j + 1], second[j : j + 1])
+        return c
+
+    lax.fori_loop(0, pairs, invert_pair, 0, unroll=3)
 
     pltpu.make_async_copy(stat_recv, stat_recv, stat_sems.at[1]).wait()
     pltpu.make_async_copy(stat_recv, stat_recv, stat_sems.at[0]).wait()
@@ -266,65 +300,69 @@
         / noise
     )
 
-    total[...] = jnp.zeros_like(total)
-
-    def unrotate_pair(p, c):
-        rows = pl.ds(pl.multiple_of(p * 8, 8), 8)
-        for j in range(tiles):
-            lane = jnp.where(
-                low_half, inverse[2 * p, j : j + 1, :], inverse[2 * p + 1, j : j + 1, :]
-            )
-            tile = jnp.where(
-                low_half,
-                inverse[2 * p, tiles + j : tiles + j + 1, :],
-                inverse[2 * p + 1, tiles + j : tiles + j + 1, :],
-            )
-            for part in range(3):
-                found = jnp.zeros((8, LANES), jnp.float32)
-                for s in range(tiles):
-                    base = part * coefs + s * LANES
-                    picked = lane_take(weighted[rows, base : base + LANES], lane)
-                    found = jnp.where(tile == s, picked, found)
-                base = part * coefs + j * LANES
-                total[:, base : base + LANES] += found
-        return c
-
-    lax.fori_loop(0, pairs, unrotate_pair, 0)
-
-    n_pieces = n_dp // 2
-    for e in range(n_pieces):
-        data = total[:, e * LANES : (e + 1) * LANES]
-        base = 2 * coefs + (e // 2) * LANES
-        mass_tile = total[:, base : base + LANES]
-        data = data + pltpu.roll(data, 4, 0)
-        mass_tile = mass_tile + pltpu.roll(mass_tile, 4, 0)
-        piece_send[e] = jnp.where(low_half, data, mass_tile)
-
-    def piece_start(o, c):
-        target = lax.rem(me_dp + o, n_dp)
+    def unrotate(firsts, j):
+        sums = [jnp.zeros((8, LANES), jnp.float32) for _ in firsts]
+        for p in range(pairs):
+            lane = inverse[p, j]
+            tile = inverse[p, tiles + j]
+            found = [jnp.zeros((8, LANES), jnp.float32) for _ in firsts]
+            for s in range(tiles):
+                here = tile == s
+                for i, first in enumerate(firsts):
+                    base = first + s * LANES
+                    picked = lane_take(weighted[p * 8 : (p + 1) * 8, base : base + LANES], lane)
+                    found[i] = jnp.where(here, picked, found[i])
+            sums = [x + y for x, y in zip(sums, found)]
+        return [x + pltpu.roll(x, 4, 0) for x in sums]
+
+    for w in range(tiles):
+        (sums,) = unrotate([2 * coefs], w)
+        piece_weight[2 * w] = jnp.where(low_half, pltpu.roll(sums, 64, 1), pltpu.roll(sums, 32, 1))
+        piece_weight[2 * w + 1] = jnp.where(low_half, sums, pltpu.roll(sums, 96, 1))
+    my_chip = lax.div(me_dp, 2)
+    my_core = lax.rem(me_dp, 2)
+
+    def pieces(j):
+        for part, sums in enumerate(unrotate([0, coefs], j)):
+            e = part * tiles + j
+            data = jnp.where(low_half, sums, pltpu.roll(sums, 64, 1))
+            both = jnp.where(lane_row < 64, data, piece_weight[e])
+            piece_send[e, 0] = both[0:4]
+            piece_send[e, 1] = both[4:8]
+
+    def piece_start(e, core):
+        target = 2 * e + core
+        slot = lax.rem(target - me_dp + n_dp, n_dp) - 1
         pltpu.make_async_remote_copy(
-            src_ref=piece_send.at[lax.div(target, 2)],
-            dst_ref=piece_recv.at[o - 1],
+            src_ref=piece_send.at[e, core],
+            dst_ref=piece_recv.at[slot],
             send_sem=piece_sems.at[0],
             recv_sem=piece_sems.at[1],
             device_id=(target, me_cls),
             device_id_type=MESH,
         ).start()
-        return c
-
-    lax.fori_loop(1, n_dp, piece_start, 0)
+
+    def chip_pieces(step, c):
+        j = lax.rem(my_chip + 1 + step, tiles)
+        pieces(j)
+        for part in range(2):
+            for core in range(2):
+                piece_start(part * tiles + j, core)
+        return c
+
+    lax.fori_loop(0, tiles - 1, chip_pieces, 0)
+    mine = lax.rem(my_chip, tiles)
+    other = lax.rem(my_chip + tiles, 2 * tiles)
+    pieces(mine)
+    piece_start(other, 0)
+    piece_start(other, 1)
+    piece_start(my_chip, 1 - my_core)
+    gathered = piece_send[my_chip, my_core]
     pltpu.make_async_copy(piece_recv, piece_recv, piece_sems.at[1]).wait()
-    gathered = piece_send[lax.div(me_dp, 2)]
     for o in range(n_dp - 1):
         gathered = gathered + piece_recv[o]
-    data_part = lax.rem(me_dp, 2)
-    weight_part = lax.rem(me_dp, 4)
-    data_out = jnp.where(data_part == 0, gathered, pltpu.roll(gathered, 64, 1))
-    data_ref[...] = data_out[0:4, :64]
-    weight_out = gathered
-    for w in range(1, 4):
-        weight_out = jnp.where(weight_part == w, pltpu.roll(gathered, LANES - 32 * w, 1), weight_out)
-    weight_ref[...] = weight_out[4:8, :32]
+    data_ref[...] = gathered[:, :64]
+    weight_ref[...] = pltpu.roll(gathered, 64, 1)[:, :32]
     pltpu.make_async_copy(piece_recv, piece_recv, piece_sems.at[0]).wait()
 
 
@@ -334,7 +372,7 @@
     n_dp = lax.axis_size("dp")
     n_cls = lax.axis_size("cls")
     padded = SHIFTS + 1
-    cosine, sine = phase_tables(coefs, padded)
+    trig = jnp.asarray(np.stack(phase_tables(coefs, padded), axis=1))
     rows = padded * slots
     pair_count = classes * TURNS
     vmem = pl.BlockSpec(memory_space=pltpu.VMEM)
@@ -345,38 +383,43 @@
             jax.ShapeDtypeStruct((classes, coefs // n_dp), jnp.float32),
             jax.ShapeDtypeStruct((1, slots), jnp.float32),
         ),
-        in_specs=[pl.BlockSpec(memory_space=pltpu.SMEM)] + [vmem] * 7,
+        in_specs=[pl.BlockSpec(memory_space=pltpu.HBM)] * 7,
         out_specs=(vmem, vmem, vmem),
         scratch_shapes=[
+            pltpu.SMEM(counts.shape, jnp.int32),
+            pltpu.VMEM(particles.shape, jnp.float32),
+            pltpu.VMEM(ctf.shape, jnp.float32),
+            pltpu.VMEM(references.shape, references.dtype),
+            pltpu.VMEM((1, coefs), jnp.float32),
+            pltpu.VMEM(rotations.shape, jnp.int32),
+            pltpu.VMEM(trig.shape, jnp.float32),
             pltpu.VMEM((slots, 2 * coefs), jnp.float32),
             pltpu.VMEM((slots, coefs), jnp.bfloat16),
             pltpu.VMEM((rows, 2 * coefs), jnp.bfloat16),
             pltpu.VMEM((pair_count, 2 * coefs), jnp.float32),
             pltpu.VMEM((pair_count, rows), jnp.float32),
             pltpu.VMEM((pair_count, 3 * coefs), jnp.float32),
-            pltpu.VMEM((TURNS, 2 * coefs // LANES, LANES), jnp.int32),
+            pltpu.VMEM((TURNS // 2, 2 * coefs // LANES, 8, LANES), jnp.int32),
             pltpu.VMEM((TURNS, 8, coefs), jnp.int32),
-            pltpu.VMEM((8, 3 * coefs), jnp.float32),
+            pltpu.VMEM((8, 2 * coefs), jnp.float32),
             pltpu.VMEM((8, LANES), jnp.float32),
             pltpu.VMEM((n_cls - 1, 8, LANES), jnp.float32),
             pltpu.VMEM((n_dp // 2, 8, LANES), jnp.float32),
-            pltpu.VMEM((n_dp - 1, 8, LANES), jnp.float32),
+            pltpu.VMEM((n_dp // 2, 2, 4, LANES), jnp.float32),
+            pltpu.VMEM((n_dp - 1, 4, LANES), jnp.float32),
+            pltpu.SemaphoreType.DMA((7,)),
             pltpu.SemaphoreType.DMA((2,)),
             pltpu.SemaphoreType.DMA((2,)),
         ],
         compiler_params=pltpu.CompilerParams(
-            collective_id=0, has_side_effects=True, vmem_limit_bytes=48 << 20
+            collective_id=0, has_side_effects=True, vmem_limit_bytes=40 << 20
         ),
         name="class_average",
     )(
-        counts,
-        particles,
-        ctf,
-        references,
-        noise.reshape(1, coefs),
-        rotations,
-        jnp.asarray(cosine),
-        jnp.asarray(sine),
+        *[
+            pltpu.with_memory_space_constraint(x, pltpu.HBM)
+            for x in (counts, particles, ctf, references, noise.reshape(1, coefs), rotations, trig)
+        ]
     )
     return data, weight, evidence.reshape(slots)
 

time: 40.4 us -> 33.9 us (0.84)
  local copies, waits for them, and re-layouts: 8.41 us -> 1.67 us
  Pallas kernels: 31 us -> 31.5 us
    unnamed x19 -> x3, local copies, waits for them, and re-layouts: 8.41 us -> 1.67 us
    pallas_call x1, Pallas kernels: 31 us -> 31.5 us  [body(): pl.pallas_call(functools.partial(kernel, (n_dp, n_cls, slots, coefs)), ou...]
where the time goes in v2:
time: 33.9 us; the launch traced here: 33.8 us
  Pallas kernels  31.5 us (93%)
  local copies, waits for them, and re-layouts  1.67 us (5%)
  between operations  0.64 us (2%)
    pallas_call x1, Pallas kernels, body(): pl.pallas_call(functools.partial(kernel, (n_dp, n_cls, slots, coefs)), ou...  31.5 us
    unnamed x3, local copies, waits for them, and re-layouts  1.67 us

profile of v2, /device:TPU:1, one launch (start us, length us, event | category | flops | bytes accessed | tf_op | source)
XLA Modules:
  0.0 33.8 jit_solution(2000730897980996639)
XLA Ops:
  0.6 31.5 %class_average.1 = (f32[4,64]{1,0:T(4,128)S(1)}, f32[4,32]{1,0:T(4,128)S(1)}, f32[1,64]{1,0:T(1,128)S(1)}) custom-call(s32[2]{0:T(128)} %counts_hbm.1, f32[64,2048]{1,0:T(8,128)} %part_hbm.1, f32[64,1024]{1,0:T(8,128)} %ctf_hbm.1, bf16[4,2048]{1,0:T(4,128)(2,1)} %refs_hbm.1, f32[1,1024]{1,0:T(1,128)} %bitcast.3, s32[18,1024]{1,0:T(8,128)} %rot_hbm.1, ...), custom_call_target="tpu_custom_call" | custom-call | tf_op jit(solution)/shard_map/class_average/pallas_call | solution.py:379
  32.1 0.6 %copy.13 = f32[4,64]{1,0:T(4,128)} copy(f32[4,64]{1,0:T(4,128)S(1)} %get-tuple-element.12) | data formatting | bytes 2048
  32.7 0.6 %copy.14 = f32[4,32]{1,0:T(4,128)} copy(f32[4,32]{1,0:T(4,128)S(1)} %get-tuple-element.13) | data formatting | bytes 1024
  33.3 0.5 %copy.15 = f32[64]{0:T(128)} copy(f32[64]{0:T(128)S(1)} %bitcast.2) | data formatting | bytes 512

commit v3 on v2

--- a/solution.py
+++ b/solution.py
@@ -17,22 +17,18 @@
 MESH = pl.DeviceIdType.MESH
 
 
-def phase_tables(coef_count, rows):
+def phase_tables(coef_count):
     coefs = np.arange(coef_count)
     freq_x = (coefs % 32).astype(np.float32)
     freq_y = (coefs // 32 - coef_count // 64).astype(np.float32)
-    offsets = np.arange(SHIFTS)
+    offsets = np.arange(SHIFTS // 2)
     step_x = (offsets // SIDE - SIDE // 2).astype(np.float32)
     step_y = (offsets % SIDE - SIDE // 2).astype(np.float32)
     angles = np.float32(2.0 * math.pi / 64.0) * (
         step_x[:, None] * freq_x[None, :] + step_y[:, None] * freq_y[None, :]
     )
     wide = angles.astype(np.float32).astype(np.float64)
-    pad = ((0, rows - SHIFTS), (0, 0))
-    return (
-        np.pad(np.cos(wide).astype(np.float32), pad),
-        np.pad(np.sin(wide).astype(np.float32), pad),
-    )
+    return np.cos(wide).astype(np.float32), np.sin(wide).astype(np.float32)
 
 
 def iota(shape, axis):
@@ -87,6 +83,8 @@
     lanes_used = SHIFTS * slots
     me_dp = lax.axis_index("dp")
     me_cls = lax.axis_index("cls")
+    my_chip = lax.div(me_dp, 2)
+    my_core = lax.rem(me_dp, 2)
 
     loads = [
         pltpu.make_async_copy(source, target, load_sems.at[i])
@@ -122,27 +120,8 @@
     lax.fori_loop(1, n_dp, greet_dp, 0)
     lax.fori_loop(1, n_cls, greet_cls, 0)
 
-    for load in loads:
-        load.wait()
-
-    noise = noise_ref[...]
-    transfer = ctf_ref[...]
-    scaled[:, :coefs] = part_ref[:, :coefs] * transfer / noise
-    scaled[:, coefs:] = part_ref[:, coefs:] * transfer / noise
-    csq[...] = (transfer * transfer).astype(jnp.bfloat16)
-
-    def one_shift(s, c):
-        cosine = trig_ref[s, 0:1, :]
-        sine = trig_ref[s, 1:2, :]
-        rows = pl.ds(pl.multiple_of(s * slots, slots), slots)
-        real = scaled[:, :coefs]
-        imag = scaled[:, coefs:]
-        shifted[rows, :coefs] = (real * cosine + imag * sine).astype(jnp.bfloat16)
-        shifted[rows, coefs:] = (imag * cosine - real * sine).astype(jnp.bfloat16)
-        return c
-
-    lax.fori_loop(0, shift_rows // slots, one_shift, 0)
-
+    loads[0].wait()
+    loads[1].wait()
     low_half = iota((8, LANES), 0) < 4
     for r in range(TURNS):
         turns[r] = jnp.broadcast_to(rot_ref[r : r + 1, :], (8, coefs))
@@ -166,7 +145,36 @@
                 rotated[rows, base : base + LANES] = found
         return c
 
-    lax.fori_loop(0, pairs, rotate_pair, 0)
+    lax.fori_loop(0, pairs, rotate_pair, 0, unroll=3)
+    for load in loads[2:]:
+        load.wait()
+
+    noise = noise_ref[...]
+    transfer = ctf_ref[...]
+    scaled[:, :coefs] = part_ref[:, :coefs] * transfer / noise
+    scaled[:, coefs:] = part_ref[:, coefs:] * transfer / noise
+    csq[...] = (transfer * transfer).astype(jnp.bfloat16)
+
+    def shift_pair(s, c):
+        cosine = trig_ref[s, 0:1, :]
+        sine = trig_ref[s, 1:2, :]
+        ahead = pl.ds(pl.multiple_of(s * slots, slots), slots)
+        back = pl.ds(pl.multiple_of((SHIFTS - 1 - s) * slots, slots), slots)
+        real = scaled[:, :coefs]
+        imag = scaled[:, coefs:]
+        real_cos = real * cosine
+        imag_sin = imag * sine
+        imag_cos = imag * cosine
+        real_sin = real * sine
+        shifted[ahead, :coefs] = (real_cos + imag_sin).astype(jnp.bfloat16)
+        shifted[back, :coefs] = (real_cos - imag_sin).astype(jnp.bfloat16)
+        shifted[ahead, coefs:] = (imag_cos - real_sin).astype(jnp.bfloat16)
+        shifted[back, coefs:] = (imag_cos + real_sin).astype(jnp.bfloat16)
+        return c
+
+    lax.fori_loop(0, SHIFTS // 2, shift_pair, 0)
+    shifted[SHIFTS // 2 * slots : (SHIFTS // 2 + 1) * slots, :] = scaled[...].astype(jnp.bfloat16)
+    shifted[lanes_used:, :] = jnp.zeros((shift_rows - lanes_used, 2 * coefs), jnp.bfloat16)
     rot_rows = rotated.shape[0]
     turned = rotated[...]
     power = (
@@ -185,27 +193,30 @@
     half_penalty = 0.5 * penalty
 
     lane_row = iota((1, LANES), 1)
-    peak = jnp.full((1, LANES), -jnp.inf, jnp.float32)
+    peaks = jnp.full((8, LANES), -jnp.inf, jnp.float32)
     chunks = shift_rows // LANES
+    cross_all = lax.dot_general(
+        shifted[:shift_rows, :], turned, contract_cols, preferred_element_type=jnp.float32
+    )
     for j in range(chunks):
-        block = shifted[j * LANES : (j + 1) * LANES, :]
-        cross = lax.dot_general(
-            turned, block, contract_cols, preferred_element_type=jnp.float32
-        )[:rot_rows]
-        values = cross - half_penalty
+        values = cross_all[j * LANES : (j + 1) * LANES, :].T[:rot_rows] - half_penalty
         if (j + 1) * LANES > lanes_used:
             values = jnp.where(j * LANES + lane_row < lanes_used, values, -1e30)
         scores[:, j * LANES : (j + 1) * LANES] = values
-        peak = jnp.maximum(peak, jnp.max(values, axis=0, keepdims=True))
+        for q in range(0, rot_rows, 8):
+            peaks = jnp.maximum(peaks, values[q : q + 8])
+    peak = jnp.max(peaks, axis=0, keepdims=True)
     peak = jnp.maximum(peak, pltpu.roll(peak, slots, 1))
-    mass = jnp.zeros((1, LANES), jnp.float32)
+    masses = jnp.zeros((8, LANES), jnp.float32)
     for j in range(chunks):
         cols = slice(j * LANES, (j + 1) * LANES)
         values = jnp.exp(scores[:, cols] - peak)
         if (j + 1) * LANES > lanes_used:
             values = jnp.where(j * LANES + lane_row < lanes_used, values, 0.0)
         scores[:, cols] = values
-        mass = mass + jnp.sum(values, axis=0, keepdims=True)
+        for q in range(0, rot_rows, 8):
+            masses = masses + values[q : q + 8]
+    mass = jnp.sum(masses, axis=0, keepdims=True)
     mass = mass + pltpu.roll(mass, slots, 1)
     stat_send[...] = jnp.where(iota((8, LANES), 0) == 0, peak, mass)
 
@@ -247,8 +258,13 @@
     def invert_pair(p, c):
         first = invert(2 * p)
         second = invert(2 * p + 1)
-        for j in range(2 * tiles):
-            inverse[p, j] = jnp.where(low_half, first[j : j + 1], second[j : j + 1])
+        for j in range(tiles):
+            step = lax.rem(j + 2 * n_dp - my_chip - 1, tiles)
+            for half in range(2):
+                row = half * tiles + j
+                inverse[p, half * tiles + step] = jnp.where(
+                    low_half, first[row : row + 1], second[row : row + 1]
+                )
         return c
 
     lax.fori_loop(0, pairs, invert_pair, 0, unroll=3)
@@ -300,11 +316,11 @@
         / noise
     )
 
-    def unrotate(firsts, j):
+    def unrotate(firsts, step):
         sums = [jnp.zeros((8, LANES), jnp.float32) for _ in firsts]
         for p in range(pairs):
-            lane = inverse[p, j]
-            tile = inverse[p, tiles + j]
+            lane = inverse[p, step]
+            tile = inverse[p, tiles + step]
             found = [jnp.zeros((8, LANES), jnp.float32) for _ in firsts]
             for s in range(tiles):
                 here = tile == s
@@ -315,15 +331,15 @@
             sums = [x + y for x, y in zip(sums, found)]
         return [x + pltpu.roll(x, 4, 0) for x in sums]
 
-    for w in range(tiles):
-        (sums,) = unrotate([2 * coefs], w)
+    for step in range(tiles):
+        w = lax.rem(my_chip + 1 + step, tiles)
+        (sums,) = unrotate([2 * coefs], step)
         piece_weight[2 * w] = jnp.where(low_half, pltpu.roll(sums, 64, 1), pltpu.roll(sums, 32, 1))
         piece_weight[2 * w + 1] = jnp.where(low_half, sums, pltpu.roll(sums, 96, 1))
-    my_chip = lax.div(me_dp, 2)
-    my_core = lax.rem(me_dp, 2)
-
-    def pieces(j):
-        for part, sums in enumerate(unrotate([0, coefs], j)):
+
+    def pieces(step):
+        j = lax.rem(my_chip + 1 + step, tiles)
+        for part, sums in enumerate(unrotate([0, coefs], step)):
             e = part * tiles + j
             data = jnp.where(low_half, sums, pltpu.roll(sums, 64, 1))
             both = jnp.where(lane_row < 64, data, piece_weight[e])
@@ -342,18 +358,14 @@
             device_id_type=MESH,
         ).start()
 
-    def chip_pieces(step, c):
+    for step in range(tiles):
+        pieces(step)
         j = lax.rem(my_chip + 1 + step, tiles)
-        pieces(j)
-        for part in range(2):
-            for core in range(2):
-                piece_start(part * tiles + j, core)
-        return c
-
-    lax.fori_loop(0, tiles - 1, chip_pieces, 0)
-    mine = lax.rem(my_chip, tiles)
+        if step < tiles - 1:
+            for part in range(2):
+                for core in range(2):
+                    piece_start(part * tiles + j, core)
     other = lax.rem(my_chip + tiles, 2 * tiles)
-    pieces(mine)
     piece_start(other, 0)
     piece_start(other, 1)
     piece_start(my_chip, 1 - my_core)
@@ -366,14 +378,25 @@
     pltpu.make_async_copy(piece_recv, piece_recv, piece_sems.at[0]).wait()
 
 
+def store(data, weight, evidence, data_out, weight_out, evidence_out, sems):
+    copies = [
+        pltpu.make_async_copy(data, data_out, sems.at[0]),
+        pltpu.make_async_copy(weight, weight_out, sems.at[1]),
+        pltpu.make_async_copy(evidence, evidence_out, sems.at[2]),
+    ]
+    for copy in copies:
+        copy.start()
+    for copy in copies:
+        copy.wait()
+
+
 def body(particles, ctf, references, noise, rotations, counts):
     slots, coefs = ctf.shape
     classes = references.shape[0]
     n_dp = lax.axis_size("dp")
     n_cls = lax.axis_size("cls")
-    padded = SHIFTS + 1
-    trig = jnp.asarray(np.stack(phase_tables(coefs, padded), axis=1))
-    rows = padded * slots
+    trig = jnp.asarray(np.stack(phase_tables(coefs), axis=1))
+    rows = (SHIFTS + 1) * slots
     pair_count = classes * TURNS
     vmem = pl.BlockSpec(memory_space=pltpu.VMEM)
     data, weight, evidence = pl.pallas_call(
@@ -421,6 +444,15 @@
             for x in (counts, particles, ctf, references, noise.reshape(1, coefs), rotations, trig)
         ]
     )
+    hbm = pl.BlockSpec(memory_space=pltpu.HBM)
+    data, weight, evidence = pl.pallas_call(
+        store,
+        out_shape=tuple(jax.ShapeDtypeStruct(x.shape, x.dtype) for x in (data, weight, evidence)),
+        in_specs=[vmem, vmem, vmem],
+        out_specs=(hbm, hbm, hbm),
+        scratch_shapes=[pltpu.SemaphoreType.DMA((3,))],
+        name="store",
+    )(*[pltpu.with_memory_space_constraint(x, pltpu.VMEM) for x in (data, weight, evidence)])
     return data, weight, evidence.reshape(slots)
 
 

time: 33.9 us -> 30.8 us (0.909)
  local copies, waits for them, and re-layouts: 1.67 us -> 0 us
  Pallas kernels: 31.5 us -> 30 us
    pallas_call x1, Pallas kernels: 31.5 us -> 29.4 us  [body(): pl.pallas_call(functools.partial(kernel, (n_dp, n_cls, slots, coefs)), ou...]
    unnamed x3 -> x0, local copies, waits for them, and re-layouts: 1.67 us -> none
    pallas_call x0 -> x1, Pallas kernels: none -> 0.61 us  [body(): pl.pallas_call(store, out_shape=tuple((jax.ShapeDtypeStruct(x.shape, x.dt...]
where the time goes in v3:
time: 30.8 us; the launch traced here: 30.7 us
  Pallas kernels  30 us (97%)
  between operations  0.64 us (2%)
    pallas_call x1, Pallas kernels, body(): pl.pallas_call(functools.partial(kernel, (n_dp, n_cls, slots, coefs)), ou...  29.4 us

profile of v3, /device:TPU:1, one launch (start us, length us, event | category | flops | bytes accessed | tf_op | source)
XLA Modules:
  0.0 30.7 jit_solution(701770704841717310)
XLA Ops:
  0.6 29.4 %class_average.1 = (f32[4,64]{1,0:T(4,128)S(1)}, f32[4,32]{1,0:T(4,128)S(1)}, f32[1,64]{1,0:T(1,128)S(1)}) custom-call(s32[2]{0:T(128)} %counts_hbm.1, f32[64,2048]{1,0:T(8,128)} %part_hbm.1, f32[64,1024]{1,0:T(8,128)} %ctf_hbm.1, bf16[4,2048]{1,0:T(4,128)(2,1)} %refs_hbm.1, f32[1,1024]{1,0:T(1,128)} %bitcast.2, s32[18,1024]{1,0:T(8,128)} %rot_hbm.1, ...), custom_call_target="tpu_custom_call" | custom-call | tf_op jit(solution)/shard_map/class_average/pallas_call | solution.py:402
  30.1 0.6 %store.1 = (f32[4,64]{1,0:T(4,128)}, f32[4,32]{1,0:T(4,128)}, f32[1,64]{1,0:T(1,128)}) custom-call(f32[4,64]{1,0:T(4,128)S(1)} %get-tuple-element.9.data, f32[4,32]{1,0:T(4,128)S(1)} %get-tuple-element.10.weight, f32[1,64]{1,0:T(1,128)S(1)} %get-tuple-element.11.evidence), custom_call_target="tpu_custom_call" | custom-call | tf_op jit(solution)/shard_map/store/pallas_call | solution.py:448

commit v4 on v3

--- a/solution.py
+++ b/solution.py
@@ -294,13 +294,6 @@
                 [values, jnp.zeros((QPAD - rot_rows, LANES), jnp.float32)], axis=0
             ).astype(jnp.bfloat16)
         )
-    posterior = jnp.concatenate(posterior, axis=1)
-    weighted[:, : 2 * coefs] = lax.dot_general(
-        posterior,
-        shifted[...],
-        (((1,), (0,)), ((), ())),
-        preferred_element_type=jnp.float32,
-    )[:rot_rows]
     occupancy = occupancy + pltpu.roll(occupancy, slots, 1)
     occupancy = jnp.where(lane_row < slots, occupancy, 0.0)
     occupancy = jnp.concatenate(
@@ -337,6 +330,13 @@
         piece_weight[2 * w] = jnp.where(low_half, pltpu.roll(sums, 64, 1), pltpu.roll(sums, 32, 1))
         piece_weight[2 * w + 1] = jnp.where(low_half, sums, pltpu.roll(sums, 96, 1))
 
+    posterior = jnp.concatenate(posterior, axis=1)
+    weighted[:, : 2 * coefs] = lax.dot_general(
+        posterior,
+        shifted[...],
+        (((1,), (0,)), ((), ())),
+        preferred_element_type=jnp.float32,
+    )[:rot_rows]
     def pieces(step):
         j = lax.rem(my_chip + 1 + step, tiles)
         for part, sums in enumerate(unrotate([0, coefs], step)):

time: 30.8 us -> 30.3 us (0.984)
  Pallas kernels: 30 us -> 29.5 us
    pallas_call x1, Pallas kernels: 29.4 us -> 28.9 us  [body(): pl.pallas_call(functools.partial(kernel, (n_dp, n_cls, slots, coefs)), ou...]
where the time goes in v4:
time: 30.3 us; the launch traced here: 30.2 us
  Pallas kernels  29.5 us (97%)
  between operations  0.64 us (2%)
    pallas_call x1, Pallas kernels, body(): pl.pallas_call(functools.partial(kernel, (n_dp, n_cls, slots, coefs)), ou...  28.9 us
    pallas_call x1, Pallas kernels, body(): pl.pallas_call(store, out_shape=tuple((jax.ShapeDtypeStruct(x.shape, x.dt...  0.61 us

profile of v4, /device:TPU:1, one launch (start us, length us, event | category | flops | bytes accessed | tf_op | source)
XLA Modules:
  0.0 30.2 jit_solution(12967160913171870805)
XLA Ops:
  0.6 28.9 %class_average.1 = (f32[4,64]{1,0:T(4,128)S(1)}, f32[4,32]{1,0:T(4,128)S(1)}, f32[1,64]{1,0:T(1,128)S(1)}) custom-call(s32[2]{0:T(128)} %counts_hbm.1, f32[64,2048]{1,0:T(8,128)} %part_hbm.1, f32[64,1024]{1,0:T(8,128)} %ctf_hbm.1, bf16[4,2048]{1,0:T(4,128)(2,1)} %refs_hbm.1, f32[1,1024]{1,0:T(1,128)} %bitcast.2, s32[18,1024]{1,0:T(8,128)} %rot_hbm.1, ...), custom_call_target="tpu_custom_call" | custom-call | tf_op jit(solution)/shard_map/class_average/pallas_call | solution.py:402
  29.6 0.6 %store.1 = (f32[4,64]{1,0:T(4,128)}, f32[4,32]{1,0:T(4,128)}, f32[1,64]{1,0:T(1,128)}) custom-call(f32[4,64]{1,0:T(4,128)S(1)} %get-tuple-element.9.data, f32[4,32]{1,0:T(4,128)S(1)} %get-tuple-element.10.weight, f32[1,64]{1,0:T(1,128)S(1)} %get-tuple-element.11.evidence), custom_call_target="tpu_custom_call" | custom-call | tf_op jit(solution)/shard_map/store/pallas_call | solution.py:448

commit v5 on v4

--- a/solution.py
+++ b/solution.py
@@ -172,7 +172,7 @@
         shifted[back, coefs:] = (imag_cos + real_sin).astype(jnp.bfloat16)
         return c
 
-    lax.fori_loop(0, SHIFTS // 2, shift_pair, 0)
+    lax.fori_loop(0, SHIFTS // 2, shift_pair, 0, unroll=2)
     shifted[SHIFTS // 2 * slots : (SHIFTS // 2 + 1) * slots, :] = scaled[...].astype(jnp.bfloat16)
     shifted[lanes_used:, :] = jnp.zeros((shift_rows - lanes_used, 2 * coefs), jnp.bfloat16)
     rot_rows = rotated.shape[0]

time: 30.3 us -> 30.9 us (1.020)
  Pallas kernels: 29.5 us -> 30.2 us
    pallas_call x1, Pallas kernels: 28.9 us -> 29.5 us  [body(): pl.pallas_call(functools.partial(kernel, (n_dp, n_cls, slots, coefs)), ou...]
where the time goes in v5:
time: 30.9 us; the launch traced here: 30.8 us
  Pallas kernels  30.2 us (98%)
  between operations  0.64 us (2%)
    pallas_call x1, Pallas kernels, body(): pl.pallas_call(functools.partial(kernel, (n_dp, n_cls, slots, coefs)), ou...  29.5 us

profile of v5, /device:TPU:1, one launch (start us, length us, event | category | flops | bytes accessed | tf_op | source)
XLA Modules:
  0.0 30.8 jit_solution(5760795246301687888)
XLA Ops:
  0.6 29.5 %class_average.1 = (f32[4,64]{1,0:T(4,128)S(1)}, f32[4,32]{1,0:T(4,128)S(1)}, f32[1,64]{1,0:T(1,128)S(1)}) custom-call(s32[2]{0:T(128)} %counts_hbm.1, f32[64,2048]{1,0:T(8,128)} %part_hbm.1, f32[64,1024]{1,0:T(8,128)} %ctf_hbm.1, bf16[4,2048]{1,0:T(4,128)(2,1)} %refs_hbm.1, f32[1,1024]{1,0:T(1,128)} %bitcast.2, s32[18,1024]{1,0:T(8,128)} %rot_hbm.1, ...), custom_call_target="tpu_custom_call" | custom-call | tf_op jit(solution)/shard_map/class_average/pallas_call | solution.py:402
  30.2 0.6 %store.1 = (f32[4,64]{1,0:T(4,128)}, f32[4,32]{1,0:T(4,128)}, f32[1,64]{1,0:T(1,128)}) custom-call(f32[4,64]{1,0:T(4,128)S(1)} %get-tuple-element.9.data, f32[4,32]{1,0:T(4,128)S(1)} %get-tuple-element.10.weight, f32[1,64]{1,0:T(1,128)S(1)} %get-tuple-element.11.evidence), custom_call_target="tpu_custom_call" | custom-call | tf_op jit(solution)/shard_map/store/pallas_call | solution.py:448

commit v6 on v4

--- a/solution.py
+++ b/solution.py
@@ -360,11 +360,12 @@
 
     for step in range(tiles):
         pieces(step)
-        j = lax.rem(my_chip + 1 + step, tiles)
-        if step < tiles - 1:
-            for part in range(2):
-                for core in range(2):
-                    piece_start(part * tiles + j, core)
+        if step in (2, 4, 6):
+            for done in range(step - 2 if step == 2 else step - 1, step + 1):
+                sent = lax.rem(my_chip + 1 + done, tiles)
+                for part in range(2):
+                    for core in range(2):
+                        piece_start(part * tiles + sent, core)
     other = lax.rem(my_chip + tiles, 2 * tiles)
     piece_start(other, 0)
     piece_start(other, 1)

time: 30.3 us -> 30.2 us (level)
  no operation moved by 1% of the time
where the time goes in v6:
time: 30.2 us; the launch traced here: 30.1 us
  Pallas kernels  29.4 us (97%)
  between operations  0.64 us (2%)
    pallas_call x1, Pallas kernels, body(): pl.pallas_call(functools.partial(kernel, (n_dp, n_cls, slots, coefs)), ou...  28.8 us
    pallas_call x1, Pallas kernels, body(): pl.pallas_call(store, out_shape=tuple((jax.ShapeDtypeStruct(x.shape, x.dt...  0.61 us

profile of v6, /device:TPU:1, one launch (start us, length us, event | category | flops | bytes accessed | tf_op | source)
XLA Modules:
  0.0 30.1 jit_solution(694672692587433533)
XLA Ops:
  0.6 28.8 %class_average.1 = (f32[4,64]{1,0:T(4,128)S(1)}, f32[4,32]{1,0:T(4,128)S(1)}, f32[1,64]{1,0:T(1,128)S(1)}) custom-call(s32[2]{0:T(128)} %counts_hbm.1, f32[64,2048]{1,0:T(8,128)} %part_hbm.1, f32[64,1024]{1,0:T(8,128)} %ctf_hbm.1, bf16[4,2048]{1,0:T(4,128)(2,1)} %refs_hbm.1, f32[1,1024]{1,0:T(1,128)} %bitcast.2, s32[18,1024]{1,0:T(8,128)} %rot_hbm.1, ...), custom_call_target="tpu_custom_call" | custom-call | tf_op jit(solution)/shard_map/class_average/pallas_call | solution.py:403
  29.5 0.6 %store.1 = (f32[4,64]{1,0:T(4,128)}, f32[4,32]{1,0:T(4,128)}, f32[1,64]{1,0:T(1,128)}) custom-call(f32[4,64]{1,0:T(4,128)S(1)} %get-tuple-element.9.data, f32[4,32]{1,0:T(4,128)S(1)} %get-tuple-element.10.weight, f32[1,64]{1,0:T(1,128)S(1)} %get-tuple-element.11.evidence), custom_call_target="tpu_custom_call" | custom-call | tf_op jit(solution)/shard_map/store/pallas_call | solution.py:449
